TPU v7x, 32 devices: a whole 2x2x4 slice. The times are simulated.
32 devices in a mesh: groups: 2 (over y), seq: 4 (over z), dp: 4 (over x, core).
Axes of the slice: x: 2, y: 2, z: 4, core: 2. Of those that a mesh axis runs over, the one named last changes fastest.
Arguments:
- inputs: bfloat16 [8, 4096, 448], P(('groups', 'dp'), 'seq'), parts along dimension 0, may hold values from -6 to 6
- cotangent: bfloat16 [8, 4096, 448], P(('groups', 'dp'), 'seq'), parts along dimension 0, may hold values from -6 to 6
- first_weight_matrix: bfloat16 [3, 448, 448], P(None, None, 'dp'), may hold values from -0.15625 to 0.15625
- weight_two: bfloat16 [3, 448, 448], P(None, None, 'dp'), may hold values from -0.15625 to 0.15625
Outputs:
- input_grad: bfloat16 [8, 4096, 448], P(('groups', 'dp'), 'seq'), parts along dimension 0
- grad_one: float32 [6, 448, 448], P('groups', None, 'dp'), parts along dimension 0
- grad_two: float32 [6, 448, 448], P('groups', None, 'dp'), parts along dimension 0
There are 2 independent parts, one for each index of `groups`. A program takes and returns all parts, laid end to end along the dimension named above; an argument that names none is the same for every part. Nothing has to cross between parts.
All inputs are finite; a program needn't handle non-finite values.
Results may differ from a plain program's by a relative error of at most 0.012.
Values may be sent and summed in bfloat16 or wider, within the bound.
No kernel may reach another device: no remote copies, remote signals or barrier semaphores. Data moves between devices by JAX's collectives and lax.ppermute only.
A program may use at most 64 MiB of HBM per device.

v0:
```python
import math
import jax
import jax.numpy as jnp
from jax import lax
from jax.sharding import PartitionSpec as P


def shifted(block, axis, distance):
    devices = range(lax.axis_size(axis))
    route = [(i - distance, i) for i in devices if i - distance in devices]
    return lax.ppermute(block, axis, route)


def gelu_slope(value):
    return jax.vjp(jax.nn.gelu, value)[1](jnp.ones_like(value))[0]


def outer_terms(left, right, factor):
    product = lax.dot_general(
        left, right, (((0,), (0,)), ((), ())), preferred_element_type=jnp.float32
    )
    return product * factor


def back_product(tap, weight):
    return lax.dot_general(
        tap, weight, (((1,), (1,)), ((), ())), preferred_element_type=jnp.float32
    )


def on_device(inputs, cotangent, first_weight_matrix, weight_two):
    chans = inputs.shape[2]
    rows = inputs.shape[0] * inputs.shape[1]
    factor = 1.0 / math.sqrt(
        inputs.shape[0] * lax.axis_size("dp") * inputs.shape[1] * lax.axis_size("seq")
    )
    full_one = lax.all_gather(first_weight_matrix, "dp", axis=2, tiled=True)
    flat_in = inputs.reshape(rows, chans)
    inputs_f = flat_in.astype(jnp.float32)
    input_activation = jax.nn.gelu(inputs_f).astype(jnp.bfloat16)
    act_before = shifted(input_activation, "seq", 2)
    act_after = shifted(input_activation, "seq", -2)
    flat_cot = cotangent.reshape(rows, chans)
    cot_later = shifted(flat_cot, "seq", -4)
    cot_earlier = shifted(flat_cot, "seq", 4)
    preactivation = jnp.dot(act_before, full_one[0], preferred_element_type=jnp.float32)
    preactivation = preactivation + jnp.dot(
        input_activation, full_one[1], preferred_element_type=jnp.float32
    )
    preactivation = preactivation + jnp.dot(
        act_after, full_one[2], preferred_element_type=jnp.float32
    )
    hidden_f = (inputs_f + preactivation).astype(jnp.bfloat16).astype(jnp.float32)
    act_one = jax.nn.gelu(hidden_f).astype(jnp.bfloat16)
    full_two = lax.all_gather(weight_two, "dp", axis=2, tiled=True)
    second_layer_taps = (cot_later, flat_cot, cot_earlier)
    delta_one = back_product(second_layer_taps[0], full_two[0])
    delta_one = delta_one + back_product(second_layer_taps[1], full_two[1])
    delta_one = delta_one + back_product(second_layer_taps[2], full_two[2])
    middle_gradient = (flat_cot.astype(jnp.float32) + gelu_slope(hidden_f) * delta_one).astype(
        jnp.bfloat16
    )
    part_two = jnp.stack(
        [outer_terms(act_one, second_layer_taps[k], factor) for k in range(3)]
    ).astype(jnp.bfloat16)
    grad_two = lax.psum(
        lax.psum_scatter(part_two, "dp", scatter_dimension=2, tiled=True).astype(jnp.float32), "seq"
    )
    grad_later = shifted(middle_gradient, "seq", -2)
    grad_earlier = shifted(middle_gradient, "seq", 2)
    first_layer_taps = (grad_later, middle_gradient, grad_earlier)
    delta_zero = back_product(first_layer_taps[0], full_one[0])
    delta_zero = delta_zero + back_product(first_layer_taps[1], full_one[1])
    delta_zero = delta_zero + back_product(first_layer_taps[2], full_one[2])
    input_grad = (middle_gradient.astype(jnp.float32) + gelu_slope(inputs_f) * delta_zero).astype(
        jnp.bfloat16
    )
    part_one = jnp.stack(
        [outer_terms(input_activation, first_layer_taps[k], factor) for k in range(3)]
    ).astype(jnp.bfloat16)
    grad_one = lax.psum(
        lax.psum_scatter(part_one, "dp", scatter_dimension=2, tiled=True).astype(jnp.float32), "seq"
    )
    return (input_grad.reshape(inputs.shape), grad_one, grad_two)


def solution(mesh):
    placed = (
        P(("groups", "dp"), "seq", None),
        P(("groups", "dp"), "seq", None),
        P(None, None, "dp"),
        P(None, None, "dp"),
    )
    return jax.shard_map(
        on_device,
        mesh=mesh,
        in_specs=placed,
        out_specs=(
            P(("groups", "dp"), "seq", None),
            P("groups", None, "dp"),
            P("groups", None, "dp"),
        ),
        check_vma=False,
    )
```

profile of v0, /device:TPU:0, one launch (start us, length us, event | category | flops | bytes accessed | tf_op | source)
XLA Modules:
  0.0 242.5 jit_solution(234301999639612765)
XLA Ops:
  7.2 0.0 copy-start.2
  7.2 0.0 all-gather.3.cloned.1.call-start
  7.2 2.2 copy.9
  9.4 0.0 all-gather.3.cloned.1.call-update
  9.4 0.0 all-gather.5.cloned.1.call-start
  9.5 2.1 copy.13
  11.6 0.0 all-gather.5.cloned.1.call-update
  11.6 0.0 reduce-scatter.9.cloned.1.call-start
  11.7 1.6 fusion.26
  13.2 6.9 %collective-permute-start = (bf16[1024,448]{0,1:T(8,128)(2,1)}, bf16[1024,448]{0,1:T(8,128)(2,1)}, u32[]{:S(2)}, u32[]{:S(2)}) collective-permute-start(bf16[1024,448]{0,1:T(8,128)(2,1)} %fusion.26), channel_id=1, source_target_pairs={{0,8},{4,12},{1,9},{5,13},{2,10},{6,14},{3,11},{7,15},{16,24},{20,... | collective-permute-start | bytes 2752520 | tf_op jit(solution)/shard_map/ppermute | solution.py:11
  20.1 1.3 collective-permute-start.1
  21.4 1.6 collective-permute-start.2
  23.0 11.0 %all-gather.3.cloned.1.call-done = bf16[3,448,448]{1,0,2:T(4,128)(2,1)} async-done(((bf16[3,448,112]{1,0,2:T(4,128)(2,1)}), bf16[3,448,448]{1,0,2:T(4,128)(2,1)}) %all-gather.3.cloned.1.call-update) | async-done | bytes 1204240 | tf_op jit(solution)/shard_map/all_gather | solution.py:37
  34.0 6.1 %fusion.88 = (bf16[1,448,448]{1,0,2:T(2,128)(2,1)S(1)}, bf16[1,448,448]{1,0,2:T(2,128)(2,1)S(1)}, bf16[1,448,448]{1,0,2:T(2,128)(2,1)}) fusion(bf16[3,448,448]{1,0,2:T(4,128)(2,1)} %all-gather.3.cloned.1.call-done), kind=kLoop, calls=%fused_computation.93 | loop fusion | bytes 2408448 | tf_op jit(solution)/shard_map/slice | solution.py:51
  40.1 17.2 %all-gather.5.cloned.1.call-done = bf16[3,448,448]{1,0,2:T(4,128)(2,1)} async-done(((bf16[3,448,112]{1,0,2:T(4,128)(2,1)}), bf16[3,448,448]{1,0,2:T(4,128)(2,1)}) %all-gather.5.cloned.1.call-update) | async-done | bytes 1204240 | tf_op jit(solution)/shard_map/all_gather | solution.py:55
  57.3 6.3 %fusion.87 = (bf16[1,448,448]{1,0,2:T(2,128)(2,1)}, bf16[1,448,448]{1,0,2:T(2,128)(2,1)}, bf16[1,448,448]{1,0,2:T(2,128)(2,1)}) fusion(bf16[3,448,448]{1,0,2:T(4,128)(2,1)} %all-gather.5.cloned.1.call-done), kind=kLoop, calls=%fused_computation.92 | loop fusion | bytes 2408448 | tf_op jit(solution)/shard_map/slice | solution.py:59
  63.6 2.4 copy.21
  66.0 2.0 copy.22
  68.0 1.9 copy.23
  69.9 3.5 %copy.24 = bf16[1,448,448]{2,1,0:T(8,128)(2,1)} copy(bf16[1,448,448]{1,0,2:T(2,128)(2,1)} %get-tuple-element.7) | data formatting | bytes 802816
  73.4 1.3 copy.25
  74.7 1.0 fusion.46
  75.7 3.1 %fusion.57 = f32[1024,448]{0,1:T(8,128)} fusion(bf16[1,448,448]{2,1,0:T(8,128)(2,1)S(1)} %copy.25, bf16[1,1024,448]{1,2,0:T(8,128)(2,1)} %param.5), kind=kOutput, calls=%fused_computation.71 | convolution fusion | flops 411041792 | bytes 3153920 | tf_op jit(solution)/shard_map/dot_general | solution.py:26
  78.8 1.9 fusion.74
  80.8 2.1 fusion.27
  82.8 0.0 copy-start.17
  82.8 2.3 fusion.40
  85.2 2.0 fusion.41
  87.2 0.2 pad_maximum_fusion.1
  87.4 1.8 copy.19
  89.2 2.5 %reshape.22 = bf16[448,1344]{1,0:T(8,128)(2,1)} reshape(bf16[448,3,448]{2,1,0:T(4,128)(2,1)S(1)} %bitcast.119) | data formatting | bytes 2408448
  91.7 0.0 reduce-scatter.9.cloned.1.call-update
  91.8 0.2 reduce-scatter.7.cloned.1.call-start
  92.0 3.2 %fusion.59 = f32[1024,448]{0,1:T(8,128)} fusion(bf16[1024,448]{0,1:T(8,128)(2,1)} %collective-permute-done.2, bf16[1,448,448]{2,1,0:T(8,128)(2,1)S(1)} %copy-done.10), kind=kOutput, calls=%fused_computation.73 | convolution fusion | flops 411041792 | bytes 3153920 | tf_op jit(solution)/shard_map/dot_general | solution.py:26
  95.2 1.3 copy.26
  96.5 0.0 copy-start.3
  96.5 4.2 %fusion.17 = bf16[1024,448]{0,1:T(8,128)(2,1)S(1)} fusion(bf16[1024,448]{0,1:T(8,128)(2,1)} %copy-done.17, f32[1024,448]{0,1:T(8,128)} %fusion.59, f32[1024,448]{0,1:T(8,128)S(1)} %copy-done.7, bf16[1024,448]{0,1:T(8,128)(2,1)} %collective-permute-done.2, bf16[1,448,448]{2,1,0:T(8,128)(2,1)S(1)} %copy.26, bf16[1,1024,448]{1,2,0:T(8,128)(2,1)} %param.5), kind=kOutput, calls=%fused_computation.27 | convolution fusion | flops 422051840 | bytes 7741440 | tf_op jit(solution)/shard_map/dot_general | solution.py:26
  100.7 4.5 %collective-permute-start.4 = (bf16[1024,448]{0,1:T(8,128)(2,1)S(1)}, bf16[1024,448]{0,1:T(8,128)(2,1)S(1)}, u32[]{:S(2)}, u32[]{:S(2)}) collective-permute-start(bf16[1024,448]{0,1:T(8,128)(2,1)S(1)} %fusion.17), channel_id=1, source_target_pairs={{0,8},{4,12},{1,9},{5,13},{2,10},{6,14},{3,11},{7,15},{16,24},{20,... | collective-permute-start | bytes 2752520 | tf_op jit(solution)/shard_map/ppermute | solution.py:11
  105.2 1.3 collective-permute-start.3
  106.5 0.8 fusion.43
  107.4 17.8 %collective-permute-done.4 = bf16[1024,448]{0,1:T(8,128)(2,1)S(1)} collective-permute-done((bf16[1024,448]{0,1:T(8,128)(2,1)S(1)}, bf16[1024,448]{0,1:T(8,128)(2,1)S(1)}, u32[]{:S(2)}, u32[]{:S(2)}) %collective-permute-start.4) | collective-permute-done | bytes 917536 | tf_op jit(solution)/shard_map/ppermute | solution.py:11
  125.2 0.8 fusion.42
  126.0 0.1 copy-done.18
  126.1 23.8 %collective-permute-done.3 = bf16[1024,448]{0,1:T(8,128)(2,1)S(1)} collective-permute-done((bf16[1024,448]{0,1:T(8,128)(2,1)S(1)}, bf16[1024,448]{0,1:T(8,128)(2,1)S(1)}, u32[]{:S(2)}, u32[]{:S(2)}) %collective-permute-start.3) | collective-permute-done | bytes 917536 | tf_op jit(solution)/shard_map/ppermute | solution.py:11
  149.9 0.9 copy-done.15
  150.8 0.8 fusion.44
  151.6 0.2 pad_maximum_fusion
  151.8 1.8 copy.17
  153.6 2.5 %reshape.20 = bf16[448,1344]{1,0:T(8,128)(2,1)} reshape(bf16[448,3,448]{2,1,0:T(4,128)(2,1)S(1)} %bitcast.120) | data formatting | bytes 2408448
  156.1 0.0 reduce-scatter.7.cloned.1.call-update
  156.2 0.6 fusion.69
  156.9 0.4 copy-done.1
  157.2 0.3 copy-done.16
  157.5 0.6 fusion.72
  158.2 0.5 copy-done.4
  158.7 0.1 copy-done.12
  158.8 0.5 copy-done.19
  159.3 2.7 %fusion.52 = bf16[1,1024,448]{1,2,0:T(8,128)(2,1)} fusion(f32[1024,448]{0,1:T(8,128)S(1)} %fusion.72, f32[1024,448]{0,1:T(8,128)S(1)} %fusion.69, bf16[1,1024,448]{1,2,0:T(8,128)(2,1)S(1)} %copy-done.4, bf16[1024,448]{0,1:T(8,128)(2,1)S(1)} %copy-done.14, bf16[1024,448]{0,1:T(8,128)(2,1)S(1)} %copy-done.19, bf16[1,448,448]{2,1,0:T(8,128)(2,1)S(1)} %copy-done.12), kind=kOutput, calls=%fused_computation.68 | convolution fusion | flops 422051840 | bytes 7741440 | tf_op jit(solution)/shard_map/dot_general | solution.py:26
  162.0 1.7 reshape.23
  163.7 0.3 copy.20
  164.0 15.7 %reduce-scatter.7.cloned.1.call-done = bf16[112,1344]{1,0:T(8,128)(2,1)} async-done(((bf16[448,1344]{1,0:T(8,128)(2,1)}), bf16[112,1344]{1,0:T(8,128)(2,1)}) %reduce-scatter.7.cloned.1.call-update) | async-done | bytes 301072
  179.8 1.7 reshape.21
  181.5 0.3 copy.18
  181.8 54.2 %all-reduce.2 = (f32[3,448,112]{2,1,0:T(8,128)}, f32[3,448,112]{2,1,0:T(8,128)}) all-reduce(bf16[3,448,112]{2,1,0:T(8,128)(2,1)S(1)} %copy.18, bf16[3,448,112]{2,1,0:T(8,128)(2,1)S(1)} %copy.20), channel_id=1, replica_groups=mesh['groups'=2,'seq'=4,'dp'=4] {'seq'}, use_global_device_ids=true, to_apply=%region_1.0 | all-reduce | flops 301056 | bytes 1806336 | tf_op jit(solution)/shard_map/psum | solution.py:81
  (34 shorter events, 0.1 us)
Async XLA Ops:
  7.2 4.5 %copy-start.2 = (bf16[1,1024,448]{1,2,0:T(8,128)(2,1)S(1)}, bf16[1,1024,448]{1,2,0:T(8,128)(2,1)}, u32[]{:S(2)}) copy-start(bf16[1,1024,448]{1,2,0:T(8,128)(2,1)} %param.4) | copy-start | bytes 2752516
  7.2 26.8 %all-gather.3.cloned.1.call-start = ((), (), s32[]{:S(2)}) async-start(), calls=%async_computation.2 | async-start | bytes 2293760 | tf_op jit(solution)/shard_map/all_gather | solution.py:37
  9.4 47.9 %all-gather.5.cloned.1.call-start = ((), (), s32[]{:S(2)}) async-start(), calls=%async_computation.3 | async-start | bytes 2293760 | tf_op jit(solution)/shard_map/all_gather | solution.py:55
  11.6 150.4 %reduce-scatter.9.cloned.1.call-start = ((), (), s32[]{:S(2)}) async-start(), calls=%async_computation.5 | async-start | bytes 1576960
  13.2 65.6 %collective-permute-start = (bf16[1024,448]{0,1:T(8,128)(2,1)}, bf16[1024,448]{0,1:T(8,128)(2,1)}, u32[]{:S(2)}, u32[]{:S(2)}) collective-permute-start(bf16[1024,448]{0,1:T(8,128)(2,1)} %fusion.26), channel_id=1, source_target_pairs={{0,8},{4,12},{1,9},{5,13},{2,10},{6,14},{3,11},{7,15},{16,24},{20,... | collective-permute-start | bytes 2752520 | tf_op jit(solution)/shard_map/ppermute | solution.py:11
  20.1 60.7 %collective-permute-start.1 = (bf16[1024,448]{0,1:T(8,128)(2,1)}, bf16[1024,448]{0,1:T(8,128)(2,1)}, u32[]{:S(2)}, u32[]{:S(2)}) collective-permute-start(bf16[1024,448]{0,1:T(8,128)(2,1)} %fusion.26), channel_id=1, source_target_pairs={{8,0},{12,4},{9,1},{13,5},{10,2},{14,6},{11,3},{15,7},{24,16},{28,... | collective-permute-start | bytes 2752520 | tf_op jit(solution)/shard_map/ppermute | solution.py:11
  21.4 63.8 %collective-permute-start.2 = (bf16[1024,448]{0,1:T(8,128)(2,1)}, bf16[1024,448]{0,1:T(8,128)(2,1)}, u32[]{:S(2)}, u32[]{:S(2)}) collective-permute-start(bf16[1024,448]{0,1:T(8,128)(2,1)} %bitcast), channel_id=1, source_target_pairs={} | collective-permute-start | bytes 2752520 | tf_op jit(solution)/shard_map/ppermute | solution.py:11
  66.0 12.8 %copy-start = (bf16[1,448,448]{2,1,0:T(8,128)(2,1)}, bf16[1,448,448]{2,1,0:T(8,128)(2,1)S(1)}, u32[]{:S(2)}) copy-start(bf16[1,448,448]{2,1,0:T(8,128)(2,1)S(1)} %copy.21) | copy-start | bytes 1204228
  68.0 5.4 %copy-start.6 = (bf16[1,448,448]{1,0,2:T(2,128)(2,1)S(1)}, bf16[1,448,448]{1,0,2:T(2,128)(2,1)}, u32[]{:S(2)}) copy-start(bf16[1,448,448]{1,0,2:T(2,128)(2,1)} %get-tuple-element.6) | copy-start | bytes 1204228
  69.9 4.8 %copy-start.8 = (bf16[1,448,448]{2,1,0:T(8,128)(2,1)S(1)}, bf16[1,448,448]{2,1,0:T(8,128)(2,1)}, u32[]{:S(2)}) copy-start(bf16[1,448,448]{2,1,0:T(8,128)(2,1)} %copy.22) | copy-start | bytes 1204228
  78.8 1.9 copy-start.11
  82.8 2.4 copy-start.17
  89.2 2.8 %copy-start.10 = (bf16[1,448,448]{2,1,0:T(8,128)(2,1)S(1)}, bf16[1,448,448]{2,1,0:T(8,128)(2,1)}, u32[]{:S(2)}) copy-start(bf16[1,448,448]{2,1,0:T(8,128)(2,1)} %copy.24) | copy-start | bytes 1204228
  91.7 3.4 %copy-start.5 = (bf16[1,448,448]{1,0,2:T(2,128)(2,1)S(1)}, bf16[1,448,448]{1,0,2:T(2,128)(2,1)}, u32[]{:S(2)}) copy-start(bf16[1,448,448]{1,0,2:T(2,128)(2,1)} %get-tuple-element.5) | copy-start | bytes 1204228
  91.7 4.8 %copy-start.7 = (f32[1024,448]{0,1:T(8,128)S(1)}, f32[1024,448]{0,1:T(8,128)}, u32[]{:S(2)}) copy-start(f32[1024,448]{0,1:T(8,128)} %fusion.57) | copy-start | bytes 5505028
  91.8 88.0 %reduce-scatter.7.cloned.1.call-start = ((), (), s32[]{:S(2)}) async-start(), calls=%async_computation.4 | async-start | bytes 1576960
  96.5 10.0 %copy-start.3 = (bf16[1,1024,448]{1,2,0:T(8,128)(2,1)S(1)}, bf16[1,1024,448]{1,2,0:T(8,128)(2,1)}, u32[]{:S(2)}) copy-start(bf16[1,1024,448]{1,2,0:T(8,128)(2,1)} %param.4) | copy-start | bytes 2752516
  100.7 6.7 %copy-start.13 = (bf16[1024,448]{0,1:T(8,128)(2,1)}, bf16[1024,448]{0,1:T(8,128)(2,1)S(1)}, u32[]{:S(2)}) copy-start(bf16[1024,448]{0,1:T(8,128)(2,1)S(1)} %fusion.17) | copy-start | bytes 2752516
  100.7 24.5 %collective-permute-start.4 = (bf16[1024,448]{0,1:T(8,128)(2,1)S(1)}, bf16[1024,448]{0,1:T(8,128)(2,1)S(1)}, u32[]{:S(2)}, u32[]{:S(2)}) collective-permute-start(bf16[1024,448]{0,1:T(8,128)(2,1)S(1)} %fusion.17), channel_id=1, source_target_pairs={{0,8},{4,12},{1,9},{5,13},{2,10},{6,14},{3,11},{7,15},{16,24},{20,... | collective-permute-start | bytes 2752520 | tf_op jit(solution)/shard_map/ppermute | solution.py:11
  105.2 44.7 %collective-permute-start.3 = (bf16[1024,448]{0,1:T(8,128)(2,1)S(1)}, bf16[1024,448]{0,1:T(8,128)(2,1)S(1)}, u32[]{:S(2)}, u32[]{:S(2)}) collective-permute-start(bf16[1024,448]{0,1:T(8,128)(2,1)S(1)} %fusion.17), channel_id=1, source_target_pairs={{8,0},{12,4},{9,1},{13,5},{10,2},{14,6},{11,3},{15,7},{24,16},{28,... | collective-permute-start | bytes 2752520 | tf_op jit(solution)/shard_map/ppermute | solution.py:11
  125.2 0.9 copy-start.18
  149.9 0.9 copy-start.15
  153.6 2.5 %copy-start.9 = (bf16[1,448,448]{2,1,0:T(8,128)(2,1)S(1)}, bf16[1,448,448]{2,1,0:T(8,128)(2,1)}, u32[]{:S(2)}) copy-start(bf16[1,448,448]{2,1,0:T(8,128)(2,1)} %copy.22) | copy-start | bytes 1204228
  153.6 2.5 %copy-start.14 = (bf16[1024,448]{0,1:T(8,128)(2,1)S(1)}, bf16[1024,448]{0,1:T(8,128)(2,1)}, u32[]{:S(2)}) copy-start(bf16[1024,448]{0,1:T(8,128)(2,1)} %copy-done.13) | copy-start | bytes 2752516
  156.2 1.0 copy-start.1
  156.2 1.3 copy-start.16
  157.5 1.2 copy-start.4
  157.5 1.3 copy-start.12
  157.5 1.8 copy-start.19
Sparse Core Ops, SparseCore 0:
  10.1 23.8 all-gather.2
  36.1 21.1 all-gather.4
  91.9 26.2 reduce-scatter.8
  156.3 23.4 reduce-scatter.6
where the time goes:
time: 243 us
  waiting for transfers between devices  85.6 us (35%)
  blocking collectives  54.2 us (22%)
  local copies, waits for them, and re-layouts  44.6 us (18%)
  matrix products  26.1 us (11%)
  starting transfers between devices  15.9 us (7%)
  between operations  14.1 us (6%)
    psum x1, blocking collectives, on_device(): lax.psum(lax.psum_scatter(part_one, 'dp', scatter_dimension=2, tiled=True...  54.2 us
    ppermute x5, waiting for transfers between devices, shifted(): return lax.ppermute(block, axis, route)  41.6 us
    unnamed x56, local copies, waits for them, and re-layouts  32.2 us
    all_gather x1, waiting for transfers between devices, on_device(): full_two = lax.all_gather(weight_two, 'dp', axis=2, tiled=True)  17.2 us
    unnamed x6, waiting for transfers between devices  15.8 us
    ppermute x5, starting transfers between devices, shifted(): return lax.ppermute(block, axis, route)  15.6 us
    dot_general x6, matrix products, back_product(): lax.dot_general(tap, weight, (((1,), (1,)), ((), ())), preferred_element_...  14.4 us
    all_gather x1, waiting for transfers between devices, on_device(): full_one = lax.all_gather(first_weight_matrix, 'dp', axis=2, tiled=True)  11 us
  transfers between devices with their start and end apart: 9, of which 5 were waited for; matrix products, arithmetic and copies ran while one was open for 24% of the time, Pallas kernels for 0%

commit v1 on v0

--- a/solution.py
+++ b/solution.py
@@ -78,9 +78,8 @@
     part_one = jnp.stack(
         [outer_terms(input_activation, first_layer_taps[k], factor) for k in range(3)]
     ).astype(jnp.bfloat16)
-    grad_one = lax.psum(
-        lax.psum_scatter(part_one, "dp", scatter_dimension=2, tiled=True).astype(jnp.float32), "seq"
-    )
+    my_tile = lax.psum_scatter(part_one, "dp", scatter_dimension=2, tiled=True).astype(jnp.float32)
+    grad_one = lax.all_gather(my_tile, axis_name="seq").sum(axis=0)
     return (input_grad.reshape(inputs.shape), grad_one, grad_two)
 
 

time: 243 us -> 283 us (1.16)
  waiting for transfers between devices: 85.6 us -> 127 us
  other arithmetic: 1.96 us -> 5.76 us
    all_gather x0 -> x1, waiting for transfers between devices: none -> 21.8 us  [on_device(): grad_one = lax.all_gather(my_tile, axis_name='seq').sum(axis=0)]
    unnamed x6 -> x7, waiting for transfers between devices: 15.8 us -> 35.4 us
    dot_general x6, matrix products: 14.4 us -> 11.4 us  [back_product(): lax.dot_general(tap, weight, (((1,), (1,)), ((), ())), preferred_element_...]
    reduce_sum x0 -> x1, other arithmetic: none -> 2.9 us  [on_device(): grad_one = lax.all_gather(my_tile, axis_name='seq').sum(axis=0)]
  transfers between devices with their start and end apart: 9 -> 10, of which waited for: 5 -> 7; matrix products, arithmetic and copies ran while one was open for 24% -> 19% of each run, Pallas kernels for 0% -> 0%
where the time goes in v1:
time: 283 us
  waiting for transfers between devices  127 us (45%)
  blocking collectives  51.4 us (18%)
  local copies, waits for them, and re-layouts  44.5 us (16%)
  matrix products  24.2 us (9%)
  starting transfers between devices  15.8 us (6%)
  between operations  14.1 us (5%)
  other arithmetic  5.76 us (2%)
    psum x1, blocking collectives, on_device(): lax.psum(lax.psum_scatter(part_two, 'dp', scatter_dimension=2, tiled=True...  51.4 us
    ppermute x5, waiting for transfers between devices, shifted(): return lax.ppermute(block, axis, route)  41.4 us
    unnamed x7, waiting for transfers between devices  35.4 us
    unnamed x56, local copies, waits for them, and re-layouts  32.1 us
    all_gather x1, waiting for transfers between devices, on_device(): grad_one = lax.all_gather(my_tile, axis_name='seq').sum(axis=0)  21.8 us
    all_gather x1, waiting for transfers between devices, on_device(): full_two = lax.all_gather(weight_two, 'dp', axis=2, tiled=True)  17.2 us
    ppermute x5, starting transfers between devices, shifted(): return lax.ppermute(block, axis, route)  15.6 us
    dot_general x6, matrix products, back_product(): lax.dot_general(tap, weight, (((1,), (1,)), ((), ())), preferred_element_...  11.4 us
  transfers between devices with their start and end apart: 10, of which 7 were waited for; matrix products, arithmetic and copies ran while one was open for 19% of the time, Pallas kernels for 0%

profile of v1, /device:TPU:0, one launch (start us, length us, event | category | flops | bytes accessed | tf_op | source)
XLA Modules:
  0.0 282.5 jit_solution(13720083953673352323)
XLA Ops:
  7.2 0.0 all-gather.5.cloned.1.call-start
  7.2 2.2 copy.9
  9.4 0.0 all-gather.5.cloned.1.call-update
  9.4 0.0 all-gather.7.cloned.1.call-start
  9.5 2.1 copy.13
  11.6 0.0 all-gather.7.cloned.1.call-update
  11.6 0.0 reduce-scatter.7.cloned.1.call-start
  11.7 1.6 fusion.26
  13.2 6.9 %collective-permute-start = (bf16[1024,448]{0,1:T(8,128)(2,1)}, bf16[1024,448]{0,1:T(8,128)(2,1)}, u32[]{:S(2)}, u32[]{:S(2)}) collective-permute-start(bf16[1024,448]{0,1:T(8,128)(2,1)} %fusion.26), channel_id=1, source_target_pairs={{0,8},{4,12},{1,9},{5,13},{2,10},{6,14},{3,11},{7,15},{16,24},{20,... | collective-permute-start | bytes 2752520 | tf_op jit(solution)/shard_map/ppermute | solution.py:11
  20.1 1.3 collective-permute-start.1
  21.4 1.6 collective-permute-start.2
  23.0 11.0 %all-gather.5.cloned.1.call-done = bf16[3,448,448]{1,0,2:T(4,128)(2,1)} async-done(((bf16[3,448,112]{1,0,2:T(4,128)(2,1)}), bf16[3,448,448]{1,0,2:T(4,128)(2,1)}) %all-gather.5.cloned.1.call-update) | async-done | bytes 1204240 | tf_op jit(solution)/shard_map/all_gather | solution.py:37
  34.0 6.1 %fusion.88 = (bf16[1,448,448]{1,0,2:T(2,128)(2,1)S(1)}, bf16[1,448,448]{1,0,2:T(2,128)(2,1)}, bf16[1,448,448]{1,0,2:T(2,128)(2,1)S(1)}) fusion(bf16[3,448,448]{1,0,2:T(4,128)(2,1)} %all-gather.5.cloned.1.call-done), kind=kLoop, calls=%fused_computation.93 | loop fusion | bytes 2408448 | tf_op jit(solution)/shard_map/slice | solution.py:51
  40.1 17.2 %all-gather.7.cloned.1.call-done = bf16[3,448,448]{1,0,2:T(4,128)(2,1)} async-done(((bf16[3,448,112]{1,0,2:T(4,128)(2,1)}), bf16[3,448,448]{1,0,2:T(4,128)(2,1)}) %all-gather.7.cloned.1.call-update) | async-done | bytes 1204240 | tf_op jit(solution)/shard_map/all_gather | solution.py:55
  57.3 6.3 %fusion.87 = (bf16[1,448,448]{1,0,2:T(2,128)(2,1)}, bf16[1,448,448]{1,0,2:T(2,128)(2,1)}, bf16[1,448,448]{1,0,2:T(2,128)(2,1)}) fusion(bf16[3,448,448]{1,0,2:T(4,128)(2,1)} %all-gather.7.cloned.1.call-done), kind=kLoop, calls=%fused_computation.92 | loop fusion | bytes 2408448 | tf_op jit(solution)/shard_map/slice | solution.py:59
  63.6 2.4 copy.22
  66.0 2.2 fusion.46
  68.3 1.3 copy.21
  69.6 2.0 copy.23
  71.6 3.5 %copy.24 = bf16[1,448,448]{2,1,0:T(8,128)(2,1)} copy(bf16[1,448,448]{1,0,2:T(2,128)(2,1)} %get-tuple-element.5) | data formatting | bytes 802816
  75.1 2.0 copy.25
  77.1 1.3 copy.26
  78.4 2.0 fusion.57
  80.4 1.9 fusion.74
  82.4 2.0 fusion.59
  84.4 2.1 fusion.27
  86.4 3.5 %fusion.17 = bf16[1024,448]{0,1:T(8,128)(2,1)S(1)} fusion(bf16[1024,448]{0,1:T(8,128)(2,1)S(1)} %fusion.27, f32[1024,448]{0,1:T(8,128)S(1)} %fusion.59, f32[1024,448]{0,1:T(8,128)S(1)} %fusion.57, bf16[1024,448]{0,1:T(8,128)(2,1)} %collective-permute-done.2, bf16[1,448,448]{2,1,0:T(8,128)(2,1)S(1)} %copy.26, bf16[1,1024,448]{1,2,0:T(8,128)(2,1)} %param.5), kind=kOutput, calls=%fused_computation.27 | convolution fusion | flops 422051840 | bytes 7741440 | tf_op jit(solution)/shard_map/dot_general | solution.py:26
  90.0 4.4 %collective-permute-start.4 = (bf16[1024,448]{0,1:T(8,128)(2,1)S(1)}, bf16[1024,448]{0,1:T(8,128)(2,1)S(1)}, u32[]{:S(2)}, u32[]{:S(2)}) collective-permute-start(bf16[1024,448]{0,1:T(8,128)(2,1)S(1)} %fusion.17), channel_id=1, source_target_pairs={{0,8},{4,12},{1,9},{5,13},{2,10},{6,14},{3,11},{7,15},{16,24},{20,... | collective-permute-start | bytes 2752520 | tf_op jit(solution)/shard_map/ppermute | solution.py:11
  94.4 1.5 collective-permute-start.3
  95.9 0.8 fusion.43
  96.7 17.7 %collective-permute-done.4 = bf16[1024,448]{0,1:T(8,128)(2,1)S(1)} collective-permute-done((bf16[1024,448]{0,1:T(8,128)(2,1)S(1)}, bf16[1024,448]{0,1:T(8,128)(2,1)S(1)}, u32[]{:S(2)}, u32[]{:S(2)}) %collective-permute-start.4) | collective-permute-done | bytes 917536 | tf_op jit(solution)/shard_map/ppermute | solution.py:11
  114.4 0.8 fusion.42
  115.2 0.1 copy-done.18
  115.3 23.7 %collective-permute-done.3 = bf16[1024,448]{0,1:T(8,128)(2,1)S(1)} collective-permute-done((bf16[1024,448]{0,1:T(8,128)(2,1)S(1)}, bf16[1024,448]{0,1:T(8,128)(2,1)S(1)}, u32[]{:S(2)}, u32[]{:S(2)}) %collective-permute-start.3) | collective-permute-done | bytes 917536 | tf_op jit(solution)/shard_map/ppermute | solution.py:11
  139.0 0.9 copy-done.14
  140.0 0.8 fusion.44
  140.8 0.2 pad_maximum_fusion
  141.0 1.8 copy.17
  142.8 2.5 reshape.22
  145.3 0.0 reduce-scatter.9.cloned.1.call-start
  145.4 2.0 fusion.40
  147.4 2.0 fusion.41
  149.4 0.2 pad_maximum_fusion.1
  149.6 1.8 copy.19
  151.4 2.5 reshape.24
  154.0 0.0 all-gather.9.cloned.1.call-start
  154.0 14.9 %reduce-scatter.7.cloned.1.call-done = bf16[112,1344]{1,0:T(8,128)(2,1)} async-done(((bf16[448,1344]{1,0:T(8,128)(2,1)}), bf16[112,1344]{1,0:T(8,128)(2,1)}) %reduce-scatter.7.cloned.1.call-update) | async-done | bytes 301072
  168.9 1.7 reshape.23
  170.7 0.3 copy.18
  171.0 0.9 all_gather.20
  171.9 0.6 fusion.69
  172.6 0.3 copy-done.1
  172.9 0.3 copy-done.15
  173.2 0.6 fusion.72
  173.9 0.5 copy-done.3
  174.4 0.1 copy-done.11
  174.5 0.3 copy-done.19
  174.8 2.7 fusion.52
  177.5 20.4 %reduce-scatter.9.cloned.1.call-done = bf16[112,1344]{1,0:T(8,128)(2,1)} async-done(((bf16[448,1344]{1,0:T(8,128)(2,1)}), bf16[112,1344]{1,0:T(8,128)(2,1)}) %reduce-scatter.9.cloned.1.call-update) | async-done | bytes 301072
  197.8 1.7 reshape.25
  199.6 0.3 copy.20
  199.9 51.4 %all-reduce.1 = f32[3,448,112]{2,1,0:T(8,128)} all-reduce(bf16[3,448,112]{2,1,0:T(8,128)(2,1)S(1)} %copy.20), channel_id=1, replica_groups=mesh['groups'=2,'seq'=4,'dp'=4] {'seq'}, use_global_device_ids=true, to_apply=%region_3.0 | all-reduce | flops 150528 | bytes 903168 | tf_op jit(solution)/shard_map/psum | solution.py:66
  251.3 21.8 %all-gather.9.cloned.1.call-done = f32[12,448,112]{2,1,0:T(8,128)} async-done(((f32[3,448,112]{2,1,0:T(8,128)}), f32[12,448,112]{2,1,0:T(8,128)}) %all-gather.9.cloned.1.call-update) | async-done | bytes 2408464 | tf_op jit(solution)/shard_map/all_gather | solution.py:82
  273.1 2.9 %reduce_sum.9 = f32[3,448,112]{2,1,0:T(8,128)} reduce(f32[4,3,448,112]{3,2,1,0:T(8,128)} %bitcast.122, f32[]{:T(128)} %constant.16.clone.1), dimensions={0}, to_apply=%region_1.0 | reduce | flops 451584 | bytes 3010564 | tf_op jit(solution)/shard_map/reduce_sum | solution.py:82
  (39 shorter events, 0.1 us)
Async XLA Ops:
  7.2 4.5 %copy-start.2 = (bf16[1,1024,448]{1,2,0:T(8,128)(2,1)S(1)}, bf16[1,1024,448]{1,2,0:T(8,128)(2,1)}, u32[]{:S(2)}) copy-start(bf16[1,1024,448]{1,2,0:T(8,128)(2,1)} %param.4) | copy-start | bytes 2752516
  7.2 26.8 %all-gather.5.cloned.1.call-start = ((), (), s32[]{:S(2)}) async-start(), calls=%async_computation.2 | async-start | bytes 2293760 | tf_op jit(solution)/shard_map/all_gather | solution.py:37
  9.4 47.9 %all-gather.7.cloned.1.call-start = ((), (), s32[]{:S(2)}) async-start(), calls=%async_computation.3 | async-start | bytes 2293760 | tf_op jit(solution)/shard_map/all_gather | solution.py:55
  11.6 157.3 %reduce-scatter.7.cloned.1.call-start = ((), (), s32[]{:S(2)}) async-start(), calls=%async_computation.5 | async-start | bytes 1576960
  13.2 67.2 %collective-permute-start = (bf16[1024,448]{0,1:T(8,128)(2,1)}, bf16[1024,448]{0,1:T(8,128)(2,1)}, u32[]{:S(2)}, u32[]{:S(2)}) collective-permute-start(bf16[1024,448]{0,1:T(8,128)(2,1)} %fusion.26), channel_id=1, source_target_pairs={{0,8},{4,12},{1,9},{5,13},{2,10},{6,14},{3,11},{7,15},{16,24},{20,... | collective-permute-start | bytes 2752520 | tf_op jit(solution)/shard_map/ppermute | solution.py:11
  20.1 64.2 %collective-permute-start.1 = (bf16[1024,448]{0,1:T(8,128)(2,1)}, bf16[1024,448]{0,1:T(8,128)(2,1)}, u32[]{:S(2)}, u32[]{:S(2)}) collective-permute-start(bf16[1024,448]{0,1:T(8,128)(2,1)} %fusion.26), channel_id=1, source_target_pairs={{8,0},{12,4},{9,1},{13,5},{10,2},{14,6},{11,3},{15,7},{24,16},{28,... | collective-permute-start | bytes 2752520 | tf_op jit(solution)/shard_map/ppermute | solution.py:11
  21.4 61.0 %collective-permute-start.2 = (bf16[1024,448]{0,1:T(8,128)(2,1)}, bf16[1024,448]{0,1:T(8,128)(2,1)}, u32[]{:S(2)}, u32[]{:S(2)}) collective-permute-start(bf16[1024,448]{0,1:T(8,128)(2,1)} %bitcast), channel_id=1, source_target_pairs={} | collective-permute-start | bytes 2752520 | tf_op jit(solution)/shard_map/ppermute | solution.py:11
  66.0 2.3 copy-start.6
  69.6 10.8 %copy-start = (bf16[1,448,448]{2,1,0:T(8,128)(2,1)}, bf16[1,448,448]{2,1,0:T(8,128)(2,1)S(1)}, u32[]{:S(2)}) copy-start(bf16[1,448,448]{2,1,0:T(8,128)(2,1)S(1)} %copy.21) | copy-start | bytes 1204228
  69.6 7.5 %copy-start.4 = (bf16[1,448,448]{1,0,2:T(2,128)(2,1)S(1)}, bf16[1,448,448]{1,0,2:T(2,128)(2,1)}, u32[]{:S(2)}) copy-start(bf16[1,448,448]{1,0,2:T(2,128)(2,1)} %get-tuple-element.3) | copy-start | bytes 1204228
  71.6 3.5 %copy-start.5 = (bf16[1,448,448]{1,0,2:T(2,128)(2,1)S(1)}, bf16[1,448,448]{1,0,2:T(2,128)(2,1)}, u32[]{:S(2)}) copy-start(bf16[1,448,448]{1,0,2:T(2,128)(2,1)} %get-tuple-element.4) | copy-start | bytes 1204228
  80.4 2.0 copy-start.8
  82.3 2.0 copy-start.9
  82.3 2.0 copy-start.10
  86.4 3.6 %copy-start.16 = (bf16[1024,448]{0,1:T(8,128)(2,1)}, bf16[1024,448]{0,1:T(8,128)(2,1)S(1)}, u32[]{:S(2)}) copy-start(bf16[1024,448]{0,1:T(8,128)(2,1)S(1)} %fusion.27) | copy-start | bytes 2752516
  90.0 6.7 %copy-start.12 = (bf16[1024,448]{0,1:T(8,128)(2,1)}, bf16[1024,448]{0,1:T(8,128)(2,1)S(1)}, u32[]{:S(2)}) copy-start(bf16[1024,448]{0,1:T(8,128)(2,1)S(1)} %fusion.17) | copy-start | bytes 2752516
  90.0 24.3 %collective-permute-start.4 = (bf16[1024,448]{0,1:T(8,128)(2,1)S(1)}, bf16[1024,448]{0,1:T(8,128)(2,1)S(1)}, u32[]{:S(2)}, u32[]{:S(2)}) collective-permute-start(bf16[1024,448]{0,1:T(8,128)(2,1)S(1)} %fusion.17), channel_id=1, source_target_pairs={{0,8},{4,12},{1,9},{5,13},{2,10},{6,14},{3,11},{7,15},{16,24},{20,... | collective-permute-start | bytes 2752520 | tf_op jit(solution)/shard_map/ppermute | solution.py:11
  94.4 44.7 %collective-permute-start.3 = (bf16[1024,448]{0,1:T(8,128)(2,1)S(1)}, bf16[1024,448]{0,1:T(8,128)(2,1)S(1)}, u32[]{:S(2)}, u32[]{:S(2)}) collective-permute-start(bf16[1024,448]{0,1:T(8,128)(2,1)S(1)} %fusion.17), channel_id=1, source_target_pairs={{8,0},{12,4},{9,1},{13,5},{10,2},{14,6},{11,3},{15,7},{24,16},{28,... | collective-permute-start | bytes 2752520 | tf_op jit(solution)/shard_map/ppermute | solution.py:11
  114.4 1.0 copy-start.18
  139.0 0.9 copy-start.14
  142.8 2.6 copy-start.17
  145.3 52.5 %reduce-scatter.9.cloned.1.call-start = ((), (), s32[]{:S(2)}) async-start(), calls=%async_computation.6 | async-start | bytes 1576960
  153.9 18.0 %copy-start.7 = (bf16[1,448,448]{2,1,0:T(8,128)(2,1)S(1)}, bf16[1,448,448]{2,1,0:T(8,128)(2,1)}, u32[]{:S(2)}) copy-start(bf16[1,448,448]{2,1,0:T(8,128)(2,1)} %copy-done.6) | copy-start | bytes 1204228
  153.9 18.0 %copy-start.13 = (bf16[1024,448]{0,1:T(8,128)(2,1)S(1)}, bf16[1024,448]{0,1:T(8,128)(2,1)}, u32[]{:S(2)}) copy-start(bf16[1024,448]{0,1:T(8,128)(2,1)} %copy-done.12) | copy-start | bytes 2752516
  154.0 119.1 %all-gather.9.cloned.1.call-start = ((), (), s32[]{:S(2)}) async-start(), calls=%async_computation.4 | async-start | bytes 3440640 | tf_op jit(solution)/shard_map/all_gather | solution.py:82
  171.9 1.0 copy-start.1
  171.9 1.3 copy-start.15
  173.2 1.2 copy-start.3
  173.2 1.3 copy-start.11
  173.2 1.6 copy-start.19
Sparse Core Ops, SparseCore 0:
  10.1 23.8 all-gather.4
  36.1 21.1 all-gather.6
  145.4 23.4 reduce-scatter.6
  171.6 26.2 reduce-scatter.8
  199.8 73.2 all-gather.8
